TPU v7x, 256 devices: a whole 4x4x8 slice. The times are simulated.
256 devices in a mesh: tok: 32 (over x, z), head: 8 (over y, core).
Axes of the slice: x: 4, y: 4, z: 8, core: 2. Of those that a mesh axis runs over, the one named last changes fastest.
Arguments:
- queries: bfloat16 [131072, 8, 1024], P('tok', 'head'), as said below
- keys: bfloat16 [131072, 8, 128], P('tok', 'head'), as said below
- basis: float32 [8, 1024, 256], P('head'), may hold values from -0.1875 to 0.1875
Outputs:
- subspace: float32 [8, 1024, 256], P('head')
- keymap: float32 [8, 128, 256], replicated
Inputs may be any that keep to these rules, and one draw needn't show every extreme that they name: `queries`: query features are correlated within a group and share a common part with the keys. `keys`: keys share a common part with the queries of the same tokens.
All inputs are finite; a program needn't handle non-finite values.
Results may differ from a plain program's by a relative error of at most 0.0007.
Values sent between devices are 32-bit elements; how exact they have to be, the bound alone decides.
No kernel may reach another device: no remote copies, remote signals or barrier semaphores. Data moves between devices by JAX's collectives and lax.ppermute only.
A program may use at most 64 MiB of HBM per device.

v0:
```python
import jax
import jax.numpy as jnp
from jax import lax
from jax.sharding import PartitionSpec as P

ridge = 0.1
eps = 1e-06
high = lax.Precision.HIGHEST


def orthonormal(image):
    inner = jnp.dot(image.T, image, precision=high)
    lower = jnp.linalg.cholesky(inner)
    return jax.scipy.linalg.solve_triangular(lower, image.T, lower=True).T


def transposed_product(left, right):
    return lax.dot_general(
        left, right, (((0,), (0,)), ((), ())), preferred_element_type=jnp.float32
    )


def on_device(queries, keys, basis):
    query_rows = queries[:, 0, :]
    key_rows = keys[:, 0, :]
    start_basis = basis[0]
    width = query_rows.shape[1]
    total = query_rows.shape[0] * lax.axis_size("tok")
    gram_part = transposed_product(query_rows, query_rows)
    cross_part = transposed_product(key_rows, query_rows)
    gram = lax.psum(gram_part, "tok") / total
    cross_block = lax.psum_scatter(cross_part, "tok", scatter_dimension=0, tiled=True) / total
    scale = jnp.trace(gram) / width + eps
    image = jnp.dot(gram, start_basis, precision=high)
    refined = orthonormal(image)
    small = jnp.dot(refined.T, jnp.dot(gram, refined, precision=high), precision=high)
    rhs = jnp.dot(cross_block, refined, precision=high)
    reduced = small / scale + ridge * jnp.eye(refined.shape[1], dtype=jnp.float32)
    factor = jnp.linalg.cholesky(reduced)
    mapped = jax.scipy.linalg.cho_solve((factor, True), rhs.T).T
    full_map = lax.all_gather(mapped, "tok", axis=0, tiled=True)
    every_map = lax.all_gather(full_map[None], "head", axis=0, tiled=True)
    return (refined[None], every_map)


def solution(mesh):
    placed = (P("tok", "head", None), P("tok", "head", None), P("head", None, None))
    return jax.shard_map(
        on_device,
        mesh=mesh,
        in_specs=placed,
        out_specs=(P("head", None, None), P()),
        check_vma=False,
    )
```

profile of v0, /device:TPU:1, one launch (start us, length us, event | category | flops | bytes accessed | tf_op | source)
XLA Modules:
  0.0 417.5 jit_solution(4209673344329434345)
XLA Ops:
  7.2 15.2 %fusion.2 = f32[1024,1024]{1,0:T(8,128)} fusion(bf16[4096,1,1024]{2,0,1:T(8,128)(2,1)} %param.4), kind=kOutput, calls=%fused_computation.6 | convolution fusion | flops 8589934592 | bytes 12582912 | tf_op jit(solution)/shard_map/dot_general | solution.py:18
  22.5 2.1 fusion
  26.6 168.6 %all-reduce.5.cloned.1.call-done = (f32[1024,1024]{1,0:T(8,128)}, f32[128,1024]{1,0:T(8,128)}) async-done(((f32[1024,1024]{1,0:T(8,128)}, f32[128,1024]{1,0:T(8,128)}), (f32[1024,1024]{1,0:T(8,128)}, f32[128,1024]{1,0:T(8,128)})) %all-reduce.5.cloned.1.call-update) | async-done | bytes 4718608 | tf_op jit(solution)/shard_map/psum | solution.py:31
  195.1 5.4 %fusion.6 = f32[1024,256]{1,0:T(8,128)S(1)} fusion(f32[1024,1024]{1,0:T(8,128)} %get-tuple-element.55, f32[1,1024,256]{2,1,0:T(8,128)S(1)} %copy-done), kind=kOutput, calls=%fused_computation.12 | convolution fusion | flops 3222274048 | bytes 6291456 | tf_op jit(solution)/shard_map/dot_general | solution.py:34
  200.5 1.8 fusion.44
  202.6 11.7 %cholesky.130 = f32[128,128]{1,0:T(8,128)S(1)} custom-call(f32[128,128]{1,0:T(8,128)S(1)} %cholesky.194), custom_call_target="Cholesky" | custom-call | tf_op jit(solution)/shard_map/jit(cholesky)/cholesky | solution.py:13
  214.3 9.8 %custom-call.22 = f32[1,128,128]{1,2,0:T(8,128)S(1)} custom-call(f32[1,128,128]{2,1,0:T(8,128)S(1)} %get-tuple-element.64), custom_call_target="InvertDiagBlocksLowerTriangular" | custom-call | tf_op jit(solution)/shard_map/jit(cholesky)/cholesky | solution.py:13
  224.6 11.7 %cholesky.147 = f32[128,128]{1,0:T(8,128)S(1)} custom-call(f32[128,128]{1,0:T(8,128)S(1)} %convolution_subtract_fusion.2), custom_call_target="Cholesky" | custom-call | tf_op jit(solution)/shard_map/jit(cholesky)/cholesky | solution.py:13
  236.7 3.2 select_reduce_fusion
  241.9 4.2 while.2
  246.1 19.7 %custom-call.19 = f32[2,128,128]{1,2,0:T(8,128)S(1)} custom-call(f32[2,128,128]{2,1,0:T(8,128)S(1)} %get-tuple-element.10), custom_call_target="InvertDiagBlocksLowerTriangular" | custom-call | tf_op jit(solution)/shard_map/jit(_solve_triangular)/triangular_solve | solution.py:14
  268.1 5.3 %fusion.4 = f32[1024,256]{1,0:T(8,128)S(1)} fusion(f32[1024,1024]{1,0:T(8,128)} %get-tuple-element.55, f32[128,1024]{1,0:T(8,128)S(1)} %fusion.22, f32[128,1024]{1,0:T(8,128)S(1)} %fusion.13), kind=kOutput, calls=%fused_computation.10 | convolution fusion | flops 3222536192 | bytes 6291456 | tf_op jit(solution)/shard_map/dot_general | solution.py:36
  274.0 1.8 fusion.10
  276.0 11.7 %cholesky.164 = f32[128,128]{1,0:T(8,128)S(1)} custom-call(f32[128,128]{1,0:T(8,128)S(1)} %cholesky.197), custom_call_target="Cholesky" | custom-call | tf_op jit(solution)/shard_map/jit(cholesky)/cholesky | solution.py:39
  287.8 9.8 %custom-call.23 = f32[1,128,128]{1,2,0:T(8,128)S(1)} custom-call(f32[1,128,128]{2,1,0:T(8,128)S(1)} %get-tuple-element.62), custom_call_target="InvertDiagBlocksLowerTriangular" | custom-call | tf_op jit(solution)/shard_map/jit(cholesky)/cholesky | solution.py:39
  298.1 11.7 %cholesky.181 = f32[128,128]{1,0:T(8,128)S(1)} custom-call(f32[128,128]{1,0:T(8,128)S(1)} %convolution_subtract_fusion.1), custom_call_target="Cholesky" | custom-call | tf_op jit(solution)/shard_map/jit(cholesky)/cholesky | solution.py:39
  313.2 4.3 %while.3 = (s32[]{:T(128)}, f32[256,256]{0,1:T(8,128)S(1)}, s32[2,2]{1,0:T(2,128)S(1)}, f32[2,128,128]{2,1,0:T(8,128)S(1)}, s32[]{:T(128)}) while((s32[]{:T(128)}, f32[256,256]{0,1:T(8,128)S(1)}, s32[2,2]{1,0:T(2,128)S(1)}, f32[2,128,128]{2,1,0:T(8,128)S(1)}, s32[]{:T(128)}) %tuple.60), condition=%wide.while_cond.1, body=%wide.while_body.1.sunk | while | flops 2 | bytes 393321 | solution.py:40
  313.8 1.4 dynamic-slice.19
  316.0 1.4 dynamic-slice.19
  317.5 19.7 %custom-call.20 = f32[2,128,128]{1,2,0:T(8,128)S(1)} custom-call(f32[2,128,128]{2,1,0:T(8,128)S(1)} %get-tuple-element.18), custom_call_target="InvertDiagBlocksLowerTriangular" | custom-call | tf_op jit(solution)/shard_map/jit(_cho_solve)/triangular_solve | solution.py:40
  337.2 1.7 fusion.15
  340.2 31.9 %all-gather.1 = f32[32,4,256]{2,1,0:T(4,128)S(1)} all-gather(f32[1,4,256]{2,1,0:T(4,128)S(1)} %maximum_bitcast_fusion), channel_id=1, replica_groups=mesh['tok'=32,'head'=8] {'tok'}, dimensions={0}, use_global_device_ids=true | all-gather | bytes 135168 | tf_op jit(solution)/shard_map/all_gather | solution.py:41
  374.3 33.7 %all-gather.4.cloned.1.call-done = f32[1024,256]{1,0:T(8,128)} async-done(((f32[128,256]{1,0:T(8,128)}), f32[1024,256]{1,0:T(8,128)}) %all-gather.4.cloned.1.call-update) | async-done | bytes 1048592 | tf_op jit(solution)/shard_map/all_gather | solution.py:42
  408.0 2.3 copy.61
  (79 shorter events, 17.0 us)
Async XLA Ops:
  7.2 188.0 %copy-start = (f32[1,1024,256]{2,1,0:T(8,128)S(1)}, f32[1,1024,256]{2,1,0:T(8,128)}, u32[]{:S(2)}) copy-start(f32[1,1024,256]{2,1,0:T(8,128)} %param.6) | copy-start | bytes 3145732
  7.2 15.3 %copy-start.2 = (bf16[4096,1,128]{2,0,1:T(8,128)(2,1)S(1)}, bf16[4096,1,128]{2,0,1:T(8,128)(2,1)}, u32[]{:S(2)}) copy-start(bf16[4096,1,128]{2,0,1:T(8,128)(2,1)} %param.5) | copy-start | bytes 3145732
  7.2 187.9 %all-reduce.5.cloned.1.call-start = ((), (), s32[]{:S(2)}) async-start(), calls=%async_computation.1 | async-start | bytes 9437184 | tf_op jit(solution)/shard_map/psum | solution.py:31
  7.2 15.2 %copy-start.1 = (bf16[4096,1,1024]{2,0,1:T(8,128)(2,1)S(1)}, bf16[4096,1,1024]{2,0,1:T(8,128)(2,1)}, u32[]{:S(2)}) copy-start(bf16[4096,1,1024]{2,0,1:T(8,128)(2,1)} %param.4) | copy-start | bytes 25165828
  24.6 0.7 copy-start.3
  24.6 383.3 %all-gather.4.cloned.1.call-start = ((), (), s32[]{:S(2)}) async-start(), calls=%async_computation | async-start | bytes 1179648 | tf_op jit(solution)/shard_map/all_gather | solution.py:42
Sparse Core Ops, SparseCore 0:
  24.8 170.3 all-reduce.4
  373.0 34.9 all-gather.3
where the time goes:
time: 423 us; the launch traced here: 418 us
  waiting for transfers between devices  202 us (48%)
  other arithmetic  112 us (26%)
  matrix products  37.9 us (9%)
  blocking collectives  31.9 us (8%)
  between operations  18.7 us (4%)
  local copies, waits for them, and re-layouts  14.8 us (3%)
    psum x1, waiting for transfers between devices, on_device(): gram = lax.psum(gram_part, 'tok') / total  169 us
    another operation x7, other arithmetic, on_device(): factor = jnp.linalg.cholesky(reduced)  34.9 us
    another operation x6, other arithmetic, orthonormal(): lower = jnp.linalg.cholesky(inner)  34 us
    all_gather x1, waiting for transfers between devices, on_device(): every_map = lax.all_gather(full_map[None], 'head', axis=0, tiled=True)  33.7 us
    all_gather x1, blocking collectives, on_device(): full_map = lax.all_gather(mapped, 'tok', axis=0, tiled=True)  31.9 us
    another operation x3, other arithmetic, orthonormal(): return jax.scipy.linalg.solve_triangular(lower, image.T, lower=True).T  19.7 us
    another operation x2, other arithmetic, on_device(): mapped = jax.scipy.linalg.cho_solve((factor, True), rhs.T).T  19.7 us
    dot_general x2, matrix products, transposed_product(): lax.dot_general(left, right, (((0,), (0,)), ((), ())), preferred_element_...  17.4 us
  transfers between devices with their start and end apart: 2, of which 2 were waited for; matrix products, arithmetic and copies ran while one was open for 0% of the time, Pallas kernels for 0%

commit v1 on v0

--- a/solution.py
+++ b/solution.py
@@ -38,7 +38,9 @@
     reduced = small / scale + ridge * jnp.eye(refined.shape[1], dtype=jnp.float32)
     factor = jnp.linalg.cholesky(reduced)
     mapped = jax.scipy.linalg.cho_solve((factor, True), rhs.T).T
-    full_map = lax.all_gather(mapped, "tok", axis=0, tiled=True)
+    full_map = jnp.concatenate(
+        lax.all_to_all(jnp.stack([mapped] * lax.axis_size("tok")), "tok", 0, 0), axis=0
+    )
     every_map = lax.all_gather(full_map[None], "head", axis=0, tiled=True)
     return (refined[None], every_map)
 

time: 423 us -> 395 us (0.934)
  blocking collectives: 31.9 us -> 15.3 us
  waiting for transfers between devices: 202 us -> 191 us
    all_gather x1 -> x0, blocking collectives: 31.9 us -> none  [on_device(): full_map = lax.all_gather(mapped, 'tok', axis=0, tiled=True)]
    all_to_all x0 -> x1, blocking collectives: none -> 15.3 us  [on_device(): lax.all_to_all(jnp.stack([mapped] * lax.axis_size('tok')), 'tok', 0, 0)]
    all_gather x1, waiting for transfers between devices: 33.7 us -> 22 us  [on_device(): every_map = lax.all_gather(full_map[None], 'head', axis=0, tiled=True)]
    another operation x20 -> x22, local copies, waits for them, and re-layouts: 8.33 us -> 9.1 us
  transfers between devices with their start and end apart: 2 -> 2, of which waited for: 2 -> 2; matrix products, arithmetic and copies ran while one was open for 0% -> 1% of each run, Pallas kernels for 0% -> 0%
where the time goes in v1:
time: 395 us; the launch traced here: 389 us
  waiting for transfers between devices  191 us (48%)
  other arithmetic  112 us (28%)
  matrix products  37.9 us (10%)
  between operations  18.7 us (5%)
  blocking collectives  15.3 us (4%)
  local copies, waits for them, and re-layouts  14.9 us (4%)
    psum x1, waiting for transfers between devices, on_device(): gram = lax.psum(gram_part, 'tok') / total  169 us
    another operation x7, other arithmetic, on_device(): factor = jnp.linalg.cholesky(reduced)  34.9 us
    another operation x6, other arithmetic, orthonormal(): lower = jnp.linalg.cholesky(inner)  34 us
    all_gather x1, waiting for transfers between devices, on_device(): every_map = lax.all_gather(full_map[None], 'head', axis=0, tiled=True)  22 us
    another operation x3, other arithmetic, orthonormal(): return jax.scipy.linalg.solve_triangular(lower, image.T, lower=True).T  19.7 us
    another operation x2, other arithmetic, on_device(): mapped = jax.scipy.linalg.cho_solve((factor, True), rhs.T).T  19.7 us
    dot_general x2, matrix products, transposed_product(): lax.dot_general(left, right, (((0,), (0,)), ((), ())), preferred_element_...  17.4 us
    all_to_all x1, blocking collectives, on_device(): lax.all_to_all(jnp.stack([mapped] * lax.axis_size('tok')), 'tok', 0, 0)  15.3 us
  transfers between devices with their start and end apart: 2, of which 2 were waited for; matrix products, arithmetic and copies ran while one was open for 1% of the time, Pallas kernels for 0%

profile of v1, /device:TPU:1, one launch (start us, length us, event | category | flops | bytes accessed | tf_op | source)
XLA Modules:
  0.0 389.3 jit_solution(14407854477507622929)
XLA Ops:
  7.2 15.2 %fusion.2 = f32[1024,1024]{1,0:T(8,128)} fusion(bf16[4096,1,1024]{2,0,1:T(8,128)(2,1)} %param.4), kind=kOutput, calls=%fused_computation.6 | convolution fusion | flops 8589934592 | bytes 12582912 | tf_op jit(solution)/shard_map/dot_general | solution.py:18
  22.5 2.1 fusion
  26.6 168.6 %all-reduce.5.cloned.1.call-done = (f32[1024,1024]{1,0:T(8,128)}, f32[128,1024]{1,0:T(8,128)}) async-done(((f32[1024,1024]{1,0:T(8,128)}, f32[128,1024]{1,0:T(8,128)}), (f32[1024,1024]{1,0:T(8,128)}, f32[128,1024]{1,0:T(8,128)})) %all-reduce.5.cloned.1.call-update) | async-done | bytes 4718608 | tf_op jit(solution)/shard_map/psum | solution.py:31
  195.1 5.4 %fusion.6 = f32[1024,256]{1,0:T(8,128)S(1)} fusion(f32[1024,1024]{1,0:T(8,128)} %get-tuple-element.55, f32[1,1024,256]{2,1,0:T(8,128)S(1)} %copy-done), kind=kOutput, calls=%fused_computation.12 | convolution fusion | flops 3222274048 | bytes 6291456 | tf_op jit(solution)/shard_map/dot_general | solution.py:34
  200.5 1.8 fusion.44
  202.6 11.7 %cholesky.130 = f32[128,128]{1,0:T(8,128)S(1)} custom-call(f32[128,128]{1,0:T(8,128)S(1)} %cholesky.194), custom_call_target="Cholesky" | custom-call | tf_op jit(solution)/shard_map/jit(cholesky)/cholesky | solution.py:13
  214.3 9.8 %custom-call.22 = f32[1,128,128]{1,2,0:T(8,128)S(1)} custom-call(f32[1,128,128]{2,1,0:T(8,128)S(1)} %get-tuple-element.64), custom_call_target="InvertDiagBlocksLowerTriangular" | custom-call | tf_op jit(solution)/shard_map/jit(cholesky)/cholesky | solution.py:13
  224.6 11.7 %cholesky.147 = f32[128,128]{1,0:T(8,128)S(1)} custom-call(f32[128,128]{1,0:T(8,128)S(1)} %convolution_subtract_fusion.2), custom_call_target="Cholesky" | custom-call | tf_op jit(solution)/shard_map/jit(cholesky)/cholesky | solution.py:13
  236.7 3.2 select_reduce_fusion
  241.9 4.2 %while.2 = (s32[]{:T(128)}, f32[256,256]{0,1:T(8,128)S(1)}, s32[2,2]{1,0:T(2,128)S(1)}, f32[2,128,128]{2,1,0:T(8,128)S(1)}, s32[]{:T(128)}) while((s32[]{:T(128)}, f32[256,256]{0,1:T(8,128)S(1)}, s32[2,2]{1,0:T(2,128)S(1)}, f32[2,128,128]{2,1,0:T(8,128)S(1)}, s32[]{:T(128)}) %tuple.47), condition=%wide.while_cond, body=%wide.while_body.sunk | while | flops 2 | bytes 393321 | solution.py:14
  246.1 19.7 %custom-call.19 = f32[2,128,128]{1,2,0:T(8,128)S(1)} custom-call(f32[2,128,128]{2,1,0:T(8,128)S(1)} %get-tuple-element.10), custom_call_target="InvertDiagBlocksLowerTriangular" | custom-call | tf_op jit(solution)/shard_map/jit(_solve_triangular)/triangular_solve | solution.py:14
  268.1 5.3 %fusion.4 = f32[1024,256]{1,0:T(8,128)S(1)} fusion(f32[1024,1024]{1,0:T(8,128)} %get-tuple-element.55, f32[128,1024]{1,0:T(8,128)S(1)} %fusion.22, f32[128,1024]{1,0:T(8,128)S(1)} %fusion.13), kind=kOutput, calls=%fused_computation.10 | convolution fusion | flops 3222536192 | bytes 6291456 | tf_op jit(solution)/shard_map/dot_general | solution.py:36
  274.0 1.8 fusion.10
  276.0 11.7 %cholesky.164 = f32[128,128]{1,0:T(8,128)S(1)} custom-call(f32[128,128]{1,0:T(8,128)S(1)} %cholesky.197), custom_call_target="Cholesky" | custom-call | tf_op jit(solution)/shard_map/jit(cholesky)/cholesky | solution.py:39
  287.8 9.8 %custom-call.23 = f32[1,128,128]{1,2,0:T(8,128)S(1)} custom-call(f32[1,128,128]{2,1,0:T(8,128)S(1)} %get-tuple-element.62), custom_call_target="InvertDiagBlocksLowerTriangular" | custom-call | tf_op jit(solution)/shard_map/jit(cholesky)/cholesky | solution.py:39
  298.1 11.7 %cholesky.181 = f32[128,128]{1,0:T(8,128)S(1)} custom-call(f32[128,128]{1,0:T(8,128)S(1)} %convolution_subtract_fusion.1), custom_call_target="Cholesky" | custom-call | tf_op jit(solution)/shard_map/jit(cholesky)/cholesky | solution.py:39
  313.2 4.3 %while.3 = (s32[]{:T(128)}, f32[256,256]{0,1:T(8,128)S(1)}, s32[2,2]{1,0:T(2,128)S(1)}, f32[2,128,128]{2,1,0:T(8,128)S(1)}, s32[]{:T(128)}) while((s32[]{:T(128)}, f32[256,256]{0,1:T(8,128)S(1)}, s32[2,2]{1,0:T(2,128)S(1)}, f32[2,128,128]{2,1,0:T(8,128)S(1)}, s32[]{:T(128)}) %tuple.60), condition=%wide.while_cond.1, body=%wide.while_body.1.sunk | while | flops 2 | bytes 393321 | solution.py:40
  313.8 1.4 dynamic-slice.19
  316.0 1.4 dynamic-slice.19
  317.5 19.7 %custom-call.20 = f32[2,128,128]{1,2,0:T(8,128)S(1)} custom-call(f32[2,128,128]{2,1,0:T(8,128)S(1)} %get-tuple-element.18), custom_call_target="InvertDiagBlocksLowerTriangular" | custom-call | tf_op jit(solution)/shard_map/jit(_cho_solve)/triangular_solve | solution.py:40
  337.2 1.7 fusion.15
  340.3 15.3 %all_to_all.5 = f32[32,4,256]{2,1,0:T(4,128)S(1)} all-to-all(f32[32,4,256]{2,1,0:T(4,128)S(1)} %stack.2), channel_id=1, replica_groups=mesh['tok'=32,'head'=8] {'tok'}, dimensions={0} | all-to-all | bytes 262144 | tf_op jit(solution)/shard_map/all_to_all | solution.py:42
  357.7 22.0 %all-gather.2.cloned.1.call-done = f32[8,128,256]{2,1,0:T(8,128)} async-done(((f32[1,128,256]{2,1,0:T(8,128)}), f32[8,128,256]{2,1,0:T(8,128)}) %all-gather.2.cloned.1.call-update) | async-done | bytes 1048592 | tf_op jit(solution)/shard_map/all_gather | solution.py:44
  379.8 2.3 copy.61
  (80 shorter events, 17.1 us)
Async XLA Ops:
  7.2 188.0 %copy-start = (f32[1,1024,256]{2,1,0:T(8,128)S(1)}, f32[1,1024,256]{2,1,0:T(8,128)}, u32[]{:S(2)}) copy-start(f32[1,1024,256]{2,1,0:T(8,128)} %param.6) | copy-start | bytes 3145732
  7.2 15.3 %copy-start.2 = (bf16[4096,1,128]{2,0,1:T(8,128)(2,1)S(1)}, bf16[4096,1,128]{2,0,1:T(8,128)(2,1)}, u32[]{:S(2)}) copy-start(bf16[4096,1,128]{2,0,1:T(8,128)(2,1)} %param.5) | copy-start | bytes 3145732
  7.2 187.9 %all-reduce.5.cloned.1.call-start = ((), (), s32[]{:S(2)}) async-start(), calls=%async_computation.2 | async-start | bytes 9437184 | tf_op jit(solution)/shard_map/psum | solution.py:31
  7.2 15.2 %copy-start.1 = (bf16[4096,1,1024]{2,0,1:T(8,128)(2,1)S(1)}, bf16[4096,1,1024]{2,0,1:T(8,128)(2,1)}, u32[]{:S(2)}) copy-start(bf16[4096,1,1024]{2,0,1:T(8,128)(2,1)} %param.4) | copy-start | bytes 25165828
  24.6 0.7 copy-start.3
  24.6 355.1 %all-gather.2.cloned.1.call-start = ((), (), s32[]{:S(2)}) async-start(), calls=%async_computation.1 | async-start | bytes 1179648 | tf_op jit(solution)/shard_map/all_gather | solution.py:44
Sparse Core Ops, SparseCore 0:
  24.8 170.3 all-reduce.4
  356.4 23.2 all-gather.1
